TPU v7x, 128 devices: a whole 4x4x4 slice. The times are simulated.
128 devices in a mesh: slab: 16 (over x_hi, y, core), head: 8 (over x_lo, z).
Axes of the slice: x: 4 (x_hi: 2, x_lo: 2; x = x_hi * 2 + x_lo), y: 4, z: 4, core: 2. Of those that a mesh axis runs over, the one named last changes fastest.
Arguments:
- section_activations: bfloat16 [448, 384, 256], P('slab'), may hold values from -6 to 6
- kernel_weight: bfloat16 [27, 384, 384], replicated, may hold values from -0.0625 to 0.0625
- packed_output_gradient: bfloat16 [256, 384, 256], P('slab', 'head'), may hold values from -6 to 6
- clip_length: int32 [32], replicated, may hold values from 1 to 27, as said below
- clip_slab_index: int32 [32], replicated, may hold values from 0 to 15, as said below
- packed_clip_order: int32 [32], replicated, may hold values from 0 to 31, each once
Outputs:
- input_grad: bfloat16 [448, 384, 256], P('slab', 'head')
- weight_grad: bfloat16 [27, 384, 384], P(None, 'slab', 'head')
Inputs may be any that keep to these rules, and one draw needn't show every extreme that they name: `clip_length`: the lengths of all clips sum to 256. `clip_slab_index`: every slab takes exactly two clips; the frames of a slab lie between 4 and 28, and in every draw one slab holds 28 frames and one holds 4. `packed_clip_order`: each clip appears once.
All inputs are finite; a program needn't handle non-finite values.
Results may differ from a plain program's by a relative error of at most 0.014.
Values may be sent and summed in bfloat16 or wider, within the bound.
A program may use at most 448 MiB of HBM per device.

v0:
```python
import functools
import math

import jax
import jax.numpy as jnp
from jax import lax
from jax.experimental import pallas as pl
from jax.experimental.pallas import tpu as pltpu
from jax.sharding import PartitionSpec as P

MESH = pl.DeviceIdType.MESH
ROWS = 16
COLS = 16
PIX = ROWS * COLS
SLOTS = 28
C = 384
OG = 48
NS = 16
NH = 8
CLS = 8
PER = 5
FD = 4
SCALE = 1.0 / math.sqrt(256 * PIX)


def clip_table(clip_length, clip_slab_index, packed_clip_order):
    ids = jnp.arange(clip_length.shape[0], dtype=jnp.int32)
    place = jnp.sum(
        jnp.where(packed_clip_order[None, :] == ids[:, None], ids[None, :], 0), axis=1
    )
    start = jnp.sum(
        jnp.where(place[None, :] < place[:, None], clip_length[None, :], 0), axis=1
    )
    same = clip_slab_index[None, :] == clip_slab_index[:, None]
    second = jnp.any(same & (ids[None, :] < ids[:, None]), axis=1)
    slabs = jnp.arange(NS, dtype=jnp.int32)[:, None]
    mine = clip_slab_index[None, :] == slabs
    vals = jnp.stack([start, clip_length])[None, None]
    pick = jnp.stack([mine & ~second[None, :], mine & second[None, :]], axis=1)
    return jnp.sum(jnp.where(pick[:, :, None, :], vals, 0), axis=3).reshape(-1)


def shifts(x, lane):
    row, col = lane // COLS, lane % COLS
    out = []
    for a in range(3):
        for b in range(3):
            dr, dc = 1 - a, 1 - b
            off = dr * COLS + dc
            if off == 0:
                out.append(x)
                continue
            moved = pltpu.roll(x, (-off) % PIX, 1)
            ok = (row + dr >= 0) & (row + dr < ROWS) & (col + dc >= 0) & (col + dc < COLS)
            out.append(jnp.where(ok, moved, jnp.zeros_like(moved)))
    return out


def body(
    tab, g, act, w, dx, dw,
    act_v, w_v, rbuf, qbuf, dbuf, gs, taps, part, psend, precv, ebuf, hbuf, osend, xbuf,
    s1, r1, s2, r2, s3, r3, s4, r4, s5, r5, la, lw, lo,
):
    ms = lax.axis_index("slab")
    mh = lax.axis_index("head")

    loads = []
    for f in range(SLOTS):
        loads.append(pltpu.make_async_copy(
            act.at[f], act_v.at[:, pl.ds(f * PIX, PIX)], la.at[f]))
    wloads = []
    for t in range(27):
        wloads.append(pltpu.make_async_copy(
            w.at[t], w_v.at[t // 9, :, pl.ds((t % 9) * C, C)], lw.at[t]))
    for cp in loads + wloads:
        cp.start()

    barrier = pltpu.get_barrier_semaphore()
    for k in range(1, NS):
        pl.semaphore_signal(barrier, inc=1, device_id={"slab": (ms + k) % NS}, device_id_type=MESH)
    for k in range(1, NH):
        pl.semaphore_signal(barrier, inc=1, device_id={"head": (mh + k) % NH}, device_id_type=MESH)
    pl.semaphore_wait(barrier, NS - 1 + NH - 1)

    def piece(d):
        return g.at[:, d // 2, :, pl.ds(pl.multiple_of((d % 2) * 128, 128), 128)]

    own = pltpu.make_async_copy(piece(ms), rbuf.at[ms], lo.at[0])
    own.start()
    first = []
    for k in range(1, NS):
        d = (ms + k) % NS
        cp = pltpu.make_async_remote_copy(
            src_ref=piece(d), dst_ref=rbuf.at[ms], send_sem=s1.at[k], recv_sem=r1.at[k],
            device_id={"slab": d}, device_id_type=MESH)
        cp.start()
        first.append(cp)
    own.wait()
    for cp in first:
        cp.wait()

    cls = ms // 2
    half = pl.ds(pl.multiple_of((ms % 2) * 128, 128), 128)
    second = []
    for k in list(range(1, NS)) + [0]:
        d = (ms + k) % NS
        p1, l1, p2 = tab[d * 4], tab[d * 4 + 1], tab[d * 4 + 2]
        o1 = (cls - p1 + 256) % CLS
        o2 = (cls - p2 + 256) % CLS
        n1 = (l1 - o1 + 7) // CLS
        for j in range(PER):
            i1 = (p1 + o1) // CLS + j
            i2 = (p2 + o2) // CLS + j - n1
            idx = jnp.where(j < n1, i1, i2)
            idx = jnp.minimum(jnp.maximum(idx, 0), 31)
            qbuf[d, j] = rbuf[idx // 2, idx % 2]
        if k:
            cp = pltpu.make_async_remote_copy(
                src_ref=qbuf.at[d], dst_ref=dbuf.at[cls, :, :, half],
                send_sem=s2.at[k], recv_sem=r2.at[k],
                device_id={"slab": d}, device_id_type=MESH)
            cp.start()
            second.append(cp)
        else:
            own = pltpu.make_async_copy(qbuf.at[d], dbuf.at[cls, :, :, half], lo.at[0])
            own.start()
            own.wait()
    for cp in second:
        cp.wait()

    p1, l1, p2, l2 = tab[ms * 4], tab[ms * 4 + 1], tab[ms * 4 + 2], tab[ms * 4 + 3]

    def age(j):
        return jnp.where(j < l1, j, j - l1)

    def place(j, _):
        one = j < l1
        p = jnp.where(one, p1 + j, p2 + j - l1)
        c = p % CLS
        n1 = (l1 - (c - p1 + 256) % CLS + 7) // CLS
        r = jnp.where(one, j // CLS, n1 + (j - l1) // CLS)
        live = j < l1 + l2
        c = jnp.where(live, c, 0)
        r = jnp.where(live, r, 0)
        x = dbuf[c, r]
        gs[j] = jnp.where(live, x, jnp.zeros_like(x))
        return 0

    lax.fori_loop(0, SLOTS, place, 0)
    for j in range(SLOTS, SLOTS + FD + 2):
        gs[j] = jnp.zeros((OG, PIX), jnp.bfloat16)

    third = []
    for k in range(1, NH):
        h = (mh + k) % NH
        cp = pltpu.make_async_remote_copy(
            src_ref=gs.at[pl.ds(h * FD, FD + 2)],
            dst_ref=ebuf.at[:, pl.ds(pl.multiple_of(mh * OG, OG), OG), :],
            send_sem=s3.at[k], recv_sem=r3.at[k],
            device_id={"head": h}, device_id_type=MESH)
        cp.start()
        third.append(cp)
    own = pltpu.make_async_copy(
        gs.at[pl.ds(mh * FD, FD + 2)],
        ebuf.at[:, pl.ds(pl.multiple_of(mh * OG, OG), OG), :], lo.at[0])
    own.start()

    lane48 = lax.broadcasted_iota(jnp.int32, (OG, PIX), 1)

    def build(f, _):
        x = gs[f]
        sh = shifts(x, lane48)
        for d in range(3):
            keep = age(f) >= d
            at = pl.ds(pl.multiple_of((f - d + 2) * PIX, PIX), PIX)
            for ab in range(9):
                v = sh[ab]
                if d:
                    v = jnp.where(keep, v, jnp.zeros_like(v))
                taps[(9 * (2 - d) + ab) * OG:(9 * (2 - d) + ab + 1) * OG, at] = v
        return 0

    lax.fori_loop(0, SLOTS + 2, build, 0)
    for cp in loads:
        cp.wait()
    part[...] = jnp.zeros_like(part)

    def mul(n, _):
        a4 = act_v[:, pl.ds(pl.multiple_of(n * 4 * PIX, 4 * PIX), 4 * PIX)]
        b4 = taps[:, pl.ds(pl.multiple_of((n * 4 + 2) * PIX, 2 * PIX), 4 * PIX)]
        part[...] += lax.dot_general(
            a4, b4, (((1,), (1,)), ((), ())), preferred_element_type=jnp.float32)
        return 0

    lax.fori_loop(0, SLOTS // 4, mul, 0)

    fourth = []
    for k in list(range(1, NS)) + [0]:
        d = (ms + k) % NS
        psend[d] = (part[pl.ds(pl.multiple_of(d * 24, 8), 24), :] * SCALE).astype(jnp.bfloat16)
        if k:
            cp = pltpu.make_async_remote_copy(
                src_ref=psend.at[d], dst_ref=precv.at[ms],
                send_sem=s4.at[k], recv_sem=r4.at[k],
                device_id={"slab": d}, device_id_type=MESH)
            cp.start()
            fourth.append(cp)
    precv[ms] = psend[ms]

    own.wait()
    for cp in third:
        cp.wait()
    for cp in wloads:
        cp.wait()
    lane384 = lax.broadcasted_iota(jnp.int32, (C, PIX), 1)

    def hbuild(f, _):
        sh = shifts(ebuf[f], lane384)
        at = pl.ds(pl.multiple_of(f * PIX, PIX), PIX)
        for ab in range(9):
            hbuf[ab * C:(ab + 1) * C, at] = sh[ab]
        return 0

    lax.fori_loop(0, FD + 2, hbuild, 0)

    def grad(f, _):
        total = jnp.zeros((C, PIX), jnp.float32)
        for d in range(3):
            at = pl.ds(pl.multiple_of((f + d) * PIX, PIX), PIX)
            y = jnp.dot(w_v[2 - d], hbuf[:, at], preferred_element_type=jnp.float32)
            if d:
                y = jnp.where(age(mh * FD + f + d) >= d, y, 0.0)
            total += y
        total = total.astype(jnp.bfloat16)
        for h in range(NH):
            osend[f, h] = total[h * OG:(h + 1) * OG]
        return 0

    fifth = []

    @pl.when(mh < SLOTS // FD)
    def _():
        lax.fori_loop(0, FD, grad, 0)
        xbuf[pl.ds(mh * FD, FD)] = osend[:, mh]
        for k in range(1, NH):
            h = (mh + k) % NH
            pltpu.make_async_remote_copy(
                src_ref=osend.at[:, h], dst_ref=xbuf.at[pl.ds(mh * FD, FD)],
                send_sem=s5.at[k], recv_sem=r5.at[k],
                device_id={"head": h}, device_id_type=MESH).start()

    for cp in fourth:
        cp.wait()
    acc = precv[0].astype(jnp.float32)
    for s in range(1, NS):
        acc += precv[s].astype(jnp.float32)
    dw[...] = acc.astype(jnp.bfloat16)

    for k in range(1, NH):
        src = (mh - k + NH) % NH
        h = (mh + k) % NH

        def out_copy():
            return pltpu.make_async_remote_copy(
                src_ref=osend.at[:, h], dst_ref=xbuf.at[pl.ds(mh * FD, FD)],
                send_sem=s5.at[k], recv_sem=r5.at[k],
                device_id={"head": h}, device_id_type=MESH)

        @pl.when(mh < SLOTS // FD)
        def _():
            out_copy().wait_send()

        @pl.when(src < SLOTS // FD)
        def _():
            out_copy().wait_recv()

    dx[...] = xbuf[pl.ds(0, SLOTS)]


def shards(act, w, g, clip_length, clip_slab_index, packed_clip_order):
    tab = clip_table(clip_length, clip_slab_index, packed_clip_order)
    bf = jnp.bfloat16
    dma = pltpu.SemaphoreType.DMA
    anyspace = pl.BlockSpec(memory_space=pl.ANY)
    vmem = pl.BlockSpec(memory_space=pltpu.VMEM)
    dx, dw = pl.pallas_call(
        body,
        out_shape=(
            jax.ShapeDtypeStruct((SLOTS, OG, PIX), bf),
            jax.ShapeDtypeStruct((24, 27 * OG), bf),
        ),
        in_specs=[pl.BlockSpec(memory_space=pltpu.SMEM), anyspace, anyspace, anyspace],
        out_specs=(vmem, vmem),
        scratch_shapes=[
            pltpu.VMEM((C, SLOTS * PIX), bf),
            pltpu.VMEM((3, C, 9 * C), bf),
            pltpu.VMEM((NS, 2, OG, 128), bf),
            pltpu.VMEM((NS, PER, OG, 128), bf),
            pltpu.VMEM((CLS, PER, OG, PIX), bf),
            pltpu.VMEM((SLOTS + FD + 2, OG, PIX), bf),
            pltpu.VMEM((27 * OG, (SLOTS + 4) * PIX), bf),
            pltpu.VMEM((C, 27 * OG), jnp.float32),
            pltpu.VMEM((NS, 24, 27 * OG), bf),
            pltpu.VMEM((NS, 24, 27 * OG), bf),
            pltpu.VMEM((FD + 2, C, PIX), bf),
            pltpu.VMEM((9 * C, (FD + 2) * PIX), bf),
            pltpu.VMEM((FD, NH, OG, PIX), bf),
            pltpu.VMEM((NH * FD, OG, PIX), bf),
            dma((NS,)), dma((NS,)), dma((NS,)), dma((NS,)), dma((NH,)), dma((NH,)),
            dma((NS,)), dma((NS,)), dma((NH,)), dma((NH,)),
            dma((SLOTS,)), dma((27,)), dma((1,)),
        ],
        compiler_params=pltpu.CompilerParams(
            collective_id=0, has_side_effects=True, vmem_limit_bytes=67043328),
    )(tab, g.reshape(2, 8, OG, PIX), act, w)
    return dx, dw.reshape(24, 27, OG).transpose(1, 0, 2)


def solution(mesh):
    return jax.shard_map(
        shards,
        mesh=mesh,
        in_specs=(P("slab", None, None), P(), P("slab", "head", None), P(), P(), P()),
        out_specs=(P("slab", "head", None), P(None, "slab", "head")),
        check_vma=False,
    )
```

profile of v0, /device:TPU:117, one launch (start us, length us, event | category | flops | bytes accessed | tf_op | source)
XLA Modules:
  0.0 84.0 jit_solution(13162434437736262050)
XLA Ops:
  0.6 0.9 %fusion.1 = pred[32]{0:T(512)(128)(4,1)S(1)} fusion(s32[32]{0:T(128)} %param.10), kind=kLoop, calls=%fused_computation.6 | loop fusion | flops 4064 | bytes 160 | tf_op jit(solution)/shard_map/reduce_or | solution.py:35
  1.6 0.8 select_reduce_fusion.2
  2.3 0.8 %select_reduce_fusion.1 = s32[32]{0:T(128)S(1)} fusion(s32[32]{0:T(128)} %param.9, s32[32]{0:T(128)S(1)} %select_reduce_fusion.2), kind=kLoop, calls=%fused_computation.1 | loop fusion | flops 3040 | bytes 384 | tf_op jit(solution)/shard_map/reduce_sum | solution.py:31
  3.2 0.7 pad_add_fusion.1
  3.8 0.7 fusion.3
  4.5 0.1 select_reduce_fusion
  4.7 0.1 copy.10
  4.8 0.6 reshape.112.tab
  5.4 74.7 %shard_map.77 = (bf16[28,48,256]{2,1,0:T(8,128)(2,1)}, bf16[24,1296]{1,0:T(8,128)(2,1)}) custom-call(s32[64]{0:T(128)} %reshape.112.tab, bf16[2,8,48,256]{3,2,1,0:T(8,128)(2,1)} %bitcast.5, bf16[28,384,256]{2,1,0:T(8,128)(2,1)} %act.1, bf16[27,384,384]{2,1,0:T(8,128)(2,1)} %w.1), custom_call_target="tpu_custom_call" | custom-call | tf_op jit(solution)/shard_map/pallas_call | solution.py:286
  80.1 1.1 %reshape.114 = bf16[24,27,48]{2,1,0:T(8,128)(2,1)S(1)} reshape(bf16[24,1296]{1,0:T(8,128)(2,1)} %get-tuple-element.5) | data formatting | bytes 124416 | tf_op jit(solution)/shard_map/reshape | solution.py:316
  81.3 0.7 copy.11
  82.0 2.0 %copy.13 = bf16[28,48,256]{2,1,0:T(8,128)(2,1)} copy(bf16[28,48,256]{2,1,0:T(8,128)(2,1)} %get-tuple-element.14) | data formatting | bytes 1376256
  (2 shorter events, 0.0 us)
where the time goes:
time: 84.3 us; the launch traced here: 84 us
  Pallas kernels  74.7 us (89%)
  local copies, waits for them, and re-layouts  4.57 us (5%)
  other arithmetic  4.02 us (5%)
    pallas_call x1, Pallas kernels, shards(): pl.pallas_call(body, out_shape=(jax.ShapeDtypeStruct((SLOTS, OG, PIX), bf...  74.7 us
    unnamed x2, local copies, waits for them, and re-layouts  2.72 us

commit v1 on v0

v1 whole, which is shorter than its diff:
```python
import functools
import math

import jax
import jax.numpy as jnp
from jax import lax
from jax.experimental import pallas as pl
from jax.experimental.pallas import tpu as pltpu
from jax.sharding import PartitionSpec as P

MESH = pl.DeviceIdType.MESH
ROWS = 16
COLS = 16
PIX = ROWS * COLS
SLOTS = 28
C = 384
OG = 48
NS = 16
NH = 8
CLS = 8
PER = 5
FD = 4
NC = 3
CH = OG // NC
CLIPS = 32
SCALE = 1.0 / math.sqrt(256 * PIX)


def clip_table(length, slab, order, pk, tab):
    def walk(k, at):
        c = order[k]
        n = length[c]
        pk[0, k] = slab[c]
        pk[1, k] = n
        pk[2, k] = at
        return at + n

    lax.fori_loop(0, CLIPS, walk, 0)

    def row(d, _):
        ka, kb = jnp.int32(0), jnp.int32(0)
        for k in range(CLIPS):
            hit = pk[0, k] == d
            kb = jnp.where(hit, ka, kb)
            ka = jnp.where(hit, k, ka)
        swap = order[ka] > order[kb]
        k1 = jnp.where(swap, kb, ka)
        k2 = jnp.where(swap, ka, kb)
        tab[d * 4] = pk[2, k1]
        tab[d * 4 + 1] = pk[1, k1]
        tab[d * 4 + 2] = pk[2, k2]
        tab[d * 4 + 3] = pk[1, k2]
        return 0

    lax.fori_loop(0, NS, row, 0)


def shifts(x, lane):
    row, col = lane // COLS, lane % COLS
    out = []
    for a in range(3):
        for b in range(3):
            dr, dc = 1 - a, 1 - b
            off = dr * COLS + dc
            if off == 0:
                out.append(x)
                continue
            moved = pltpu.roll(x, (-off) % PIX, 1)
            ok = (row + dr >= 0) & (row + dr < ROWS) & (col + dc >= 0) & (col + dc < COLS)
            out.append(jnp.where(ok, moved, jnp.zeros_like(moved)))
    return out


def body(
    length, slab, order, g, act, w, dx, dw,
    pk, tab, pick, act_v, w_v, rbuf0, rbuf1, rbuf2, qbuf, dbuf0, dbuf1, dbuf2, gs, taps, part, psend, precv, ebuf, hbuf, osend, xbuf,
    s1, r1, s2, r2, s3, r3, s4, r4, s5, r5, la, lw, lo,
):
    ms = lax.axis_index("slab")
    mh = lax.axis_index("head")

    loads = []
    for f in range(SLOTS):
        loads.append(pltpu.make_async_copy(
            act.at[f], act_v.at[:, pl.ds(f * PIX, PIX)], la.at[f]))
    wloads = []
    for t in range(27):
        wloads.append(pltpu.make_async_copy(
            w.at[t], w_v.at[t // 9, :, pl.ds((t % 9) * C, C)], lw.at[t]))
    for cp in loads + wloads:
        cp.start()

    barrier = pltpu.get_barrier_semaphore()
    for k in range(1, NS):
        pl.semaphore_signal(barrier, inc=1, device_id={"slab": (ms + k) % NS}, device_id_type=MESH)
    for k in range(1, NH):
        pl.semaphore_signal(barrier, inc=1, device_id={"head": (mh + k) % NH}, device_id_type=MESH)
    pl.semaphore_wait(barrier, NS - 1 + NH - 1)

    def piece(d, cs):
        return g.at[:, d // 2, cs, pl.ds(pl.multiple_of((d % 2) * 128, 128), 128)]

    rbuf, dbuf = (rbuf0, rbuf1, rbuf2), (dbuf0, dbuf1, dbuf2)
    chunks = [pl.ds(c * CH, CH) for c in range(NC)]
    own = []
    for c in range(NC):
        cp = pltpu.make_async_copy(piece(ms, chunks[c]), rbuf[c].at[ms], lo.at[c])
        cp.start()
        own.append(cp)
    first = []
    for c in range(NC):
        for k in range(1, NS):
            d = (ms + k) % NS
            cp = pltpu.make_async_remote_copy(
                src_ref=piece(d, chunks[c]), dst_ref=rbuf[c].at[ms],
                send_sem=s1.at[c, k], recv_sem=r1.at[c, k],
                device_id={"slab": d}, device_id_type=MESH)
            cp.start()
            first.append(cp)

    clip_table(length, slab, order, pk, tab)
    cls = ms // 2
    half = pl.ds(pl.multiple_of((ms % 2) * 128, 128), 128)

    def choose(d, _):
        p1, l1, p2 = tab[d * 4], tab[d * 4 + 1], tab[d * 4 + 2]
        o1 = (cls - p1 + 256) % CLS
        o2 = (cls - p2 + 256) % CLS
        n1 = (l1 - o1 + 7) // CLS
        for j in range(PER):
            i1 = (p1 + o1) // CLS + j
            i2 = (p2 + o2) // CLS + j - n1
            idx = jnp.where(j < n1, i1, i2)
            pick[d * PER + j] = jnp.minimum(jnp.maximum(idx, 0), 31)
        return 0

    lax.fori_loop(0, NS, choose, 0)
    for cp in own:
        cp.wait()
    second = []
    for c in range(NC):
        for cp in first[c * (NS - 1):(c + 1) * (NS - 1)]:
            cp.wait_recv()
        for k in list(range(1, NS)) + [0]:
            d = (ms + k) % NS
            for j in range(PER):
                idx = pick[d * PER + j]
                qbuf[d, j, c * CH:(c + 1) * CH] = rbuf[c][idx // 2, idx % 2]
            if k:
                cp = pltpu.make_async_remote_copy(
                    src_ref=qbuf.at[d, :, chunks[c], :],
                    dst_ref=dbuf[c].at[cls, :, :, half],
                    send_sem=s2.at[c, k], recv_sem=r2.at[c, k],
                    device_id={"slab": d}, device_id_type=MESH)
                cp.start()
                second.append(cp)
    own = []
    for c in range(NC):
        cp = pltpu.make_async_copy(
            qbuf.at[ms, :, chunks[c], :], dbuf[c].at[cls, :, :, half], lo.at[c])
        cp.start()
        own.append(cp)
    for cp in own:
        cp.wait()

    p1, l1, p2, l2 = tab[ms * 4], tab[ms * 4 + 1], tab[ms * 4 + 2], tab[ms * 4 + 3]

    def age(j):
        return jnp.where(j < l1, j, j - l1)

    low = mh < SLOTS // FD
    lane = lax.broadcasted_iota(jnp.int32, (CH, PIX), 1)
    third = []
    for c in range(NC):
        cs = slice(c * CH, (c + 1) * CH)
        for cp in second[c * (NS - 1):(c + 1) * (NS - 1)]:
            cp.wait_recv()

        def place(j, _):
            one = j < l1
            p = jnp.where(one, p1 + j, p2 + j - l1)
            q = p % CLS
            n1 = (l1 - (q - p1 + 256) % CLS + 7) // CLS
            r = jnp.where(one, j // CLS, n1 + (j - l1) // CLS)
            live = j < l1 + l2
            q = jnp.where(live, q, 0)
            r = jnp.where(live, r, 0)
            x = dbuf[c][q, r]
            gs[j, cs] = jnp.where(live, x, jnp.zeros_like(x))
            return 0

        lax.fori_loop(0, SLOTS, place, 0)
        if c == 0:
            for j in range(SLOTS, SLOTS + FD + 2):
                gs[j] = jnp.zeros((OG, PIX), jnp.bfloat16)

        for k in range(1, NH):
            h = (mh + k) % NH
            cp = pltpu.make_async_remote_copy(
                src_ref=gs.at[pl.ds(h * FD, FD + 2), chunks[c], :],
                dst_ref=ebuf.at[:, pl.ds(pl.multiple_of(mh * OG + c * CH, CH), CH), :],
                send_sem=s3.at[c, k], recv_sem=r3.at[c, k],
                device_id={"head": h}, device_id_type=MESH)
            third.append((h, cp))

            @pl.when(h < SLOTS // FD)
            def _(cp=cp):
                cp.start()

        def build(f, _):
            x = gs[f, cs]
            sh = shifts(x, lane)
            for d in range(3):
                keep = age(f) >= d
                at = pl.ds(pl.multiple_of((f - d + 2) * PIX, PIX), PIX)
                for ab in range(9):
                    v = sh[ab]
                    if d:
                        v = jnp.where(keep, v, jnp.zeros_like(v))
                    t = 9 * (2 - d) + ab
                    taps[(c * 27 + t) * CH:(c * 27 + t + 1) * CH, at] = v
            return 0

        lax.fori_loop(0, SLOTS + 2, build, 0, unroll=5)
    own3 = pltpu.make_async_copy(
        gs.at[pl.ds(mh * FD, FD + 2)],
        ebuf.at[:, pl.ds(pl.multiple_of(mh * OG, OG), OG), :], lo.at[0])
    own3.start()

    for cp in loads:
        cp.wait()
    part[...] = jnp.zeros_like(part)

    def mul(n, _):
        a4 = act_v[:, pl.ds(pl.multiple_of(n * 4 * PIX, 4 * PIX), 4 * PIX)]
        b4 = taps[:, pl.ds(pl.multiple_of((n * 4 + 2) * PIX, 2 * PIX), 4 * PIX)]
        part[...] += lax.dot_general(
            a4, b4, (((1,), (1,)), ((), ())), preferred_element_type=jnp.float32)
        return 0

    lax.fori_loop(0, SLOTS // 4, mul, 0)

    fourth = []
    for k in list(range(1, NS)) + [0]:
        d = (ms + k) % NS
        psend[d] = (part[pl.ds(pl.multiple_of(d * 24, 8), 24), :] * SCALE).astype(jnp.bfloat16)
        if k:
            cp = pltpu.make_async_remote_copy(
                src_ref=psend.at[d], dst_ref=precv.at[ms],
                send_sem=s4.at[k], recv_sem=r4.at[k],
                device_id={"slab": d}, device_id_type=MESH)
            cp.start()
            fourth.append(cp)
    precv[ms] = psend[ms]

    own3.wait()
    for cp in wloads:
        cp.wait()
    lane384 = lax.broadcasted_iota(jnp.int32, (C, PIX), 1)

    def hbuild(f, _):
        sh = shifts(ebuf[f], lane384)
        at = pl.ds(pl.multiple_of(f * PIX, PIX), PIX)
        for ab in range(9):
            hbuf[ab * C:(ab + 1) * C, at] = sh[ab]
        return 0

    def grad(f, _):
        total = jnp.zeros((C, PIX), jnp.float32)
        for d in range(3):
            at = pl.ds(pl.multiple_of((f + d) * PIX, PIX), PIX)
            y = jnp.dot(w_v[2 - d], hbuf[:, at], preferred_element_type=jnp.float32)
            if d:
                y = jnp.where(age(mh * FD + f + d) >= d, y, 0.0)
            total += y
        total = total.astype(jnp.bfloat16)
        for h in range(NH):
            osend[f, h] = total[h * OG:(h + 1) * OG]
        for k in range(1, NH):
            out_copy(k, f).start()
        return 0

    def out_copy(k, f):
        h = (mh + k) % NH
        return pltpu.make_async_remote_copy(
            src_ref=osend.at[f, h], dst_ref=xbuf.at[mh * FD + f],
            send_sem=s5.at[k, f], recv_sem=r5.at[k, f],
            device_id={"head": h}, device_id_type=MESH)

    @pl.when(low)
    def _():
        for _, cp in third:
            cp.wait_recv()
        lax.fori_loop(0, FD + 2, hbuild, 0)
        lax.fori_loop(0, FD, grad, 0)
        xbuf[pl.ds(mh * FD, FD)] = osend[:, mh]

    for cp in fourth:
        cp.wait()
    acc = precv[0].astype(jnp.float32)
    for s in range(1, NS):
        acc += precv[s].astype(jnp.float32)
    acc = acc.astype(jnp.bfloat16)
    for c in range(NC):
        for t in range(27):
            dw[t, :, c * CH:(c + 1) * CH] = acc[:, (c * 27 + t) * CH:(c * 27 + t + 1) * CH]

    for cp in first + second:
        cp.wait_send()
    for h, cp in third:
        @pl.when(h < SLOTS // FD)
        def _(cp=cp):
            cp.wait_send()

    @pl.when(low)
    def _():
        for k in range(1, NH):
            for f in range(FD):
                out_copy(k, f).wait_send()

    for k in range(1, NH):
        @pl.when((mh - k + NH) % NH < SLOTS // FD)
        def _(k=k):
            for f in range(FD):
                out_copy(k, f).wait_recv()

    dx[...] = xbuf[pl.ds(0, SLOTS)]


def shards(act, w, g, clip_length, clip_slab_index, packed_clip_order):
    bf = jnp.bfloat16
    dma = pltpu.SemaphoreType.DMA
    anyspace = pl.BlockSpec(memory_space=pl.ANY)
    vmem = pl.BlockSpec(memory_space=pltpu.VMEM)
    dx, dw = pl.pallas_call(
        body,
        out_shape=(
            jax.ShapeDtypeStruct((SLOTS, OG, PIX), bf),
            jax.ShapeDtypeStruct((27, 24, OG), bf),
        ),
        in_specs=[pl.BlockSpec(memory_space=pltpu.SMEM)] * 3 + [anyspace, anyspace, anyspace],
        out_specs=(vmem, vmem),
        scratch_shapes=[
            pltpu.SMEM((3, CLIPS), jnp.int32),
            pltpu.SMEM((NS * 4,), jnp.int32),
            pltpu.SMEM((NS * PER,), jnp.int32),
            pltpu.VMEM((C, SLOTS * PIX), bf),
            pltpu.VMEM((3, C, 9 * C), bf),
            *[pltpu.VMEM((NS, 2, CH, 128), bf) for _ in range(NC)],
            pltpu.VMEM((NS, PER, OG, 128), bf),
            *[pltpu.VMEM((CLS, PER, CH, PIX), bf) for _ in range(NC)],
            pltpu.VMEM((SLOTS + FD + 2, OG, PIX), bf),
            pltpu.VMEM((27 * OG, (SLOTS + 4) * PIX), bf),
            pltpu.VMEM((C, 27 * OG), jnp.float32),
            pltpu.VMEM((NS, 24, 27 * OG), bf),
            pltpu.VMEM((NS, 24, 27 * OG), bf),
            pltpu.VMEM((FD + 2, C, PIX), bf),
            pltpu.VMEM((9 * C, (FD + 2) * PIX), bf),
            pltpu.VMEM((FD, NH, OG, PIX), bf),
            pltpu.VMEM((NH * FD, OG, PIX), bf),
            dma((NC, NS)), dma((NC, NS)), dma((NC, NS)), dma((NC, NS)),
            dma((NC, NH)), dma((NC, NH)), dma((NS,)), dma((NS,)),
            dma((NH, FD)), dma((NH, FD)),
            dma((SLOTS,)), dma((27,)), dma((NC,)),
        ],
        compiler_params=pltpu.CompilerParams(
            collective_id=0, has_side_effects=True, vmem_limit_bytes=67043328),
    )(clip_length, clip_slab_index, packed_clip_order, g.reshape(2, 8, OG, PIX), act, w)
    return dx, dw


def solution(mesh):
    return jax.shard_map(
        shards,
        mesh=mesh,
        in_specs=(P("slab", None, None), P(), P("slab", "head", None), P(), P(), P()),
        out_specs=(P("slab", "head", None), P(None, "slab", "head")),
        check_vma=False,
    )
```

time: 84.3 us -> 72.1 us (0.86)
  the two profiles are of different devices: /device:TPU:117 before, /device:TPU:1 now
where the time goes in v1:
time: 72.1 us; the launch traced here: 71.9 us
  Pallas kernels  67.7 us (94%)
  local copies, waits for them, and re-layouts  3.59 us (5%)
    pallas_call x1, Pallas kernels, shards(): pl.pallas_call(body, out_shape=(jax.ShapeDtypeStruct((SLOTS, OG, PIX), bf...  67.7 us
    unnamed x2, local copies, waits for them, and re-layouts  3.59 us

profile of v1, /device:TPU:1, one launch (start us, length us, event | category | flops | bytes accessed | tf_op | source)
XLA Modules:
  0.0 71.9 jit_solution(46872140670008653)
XLA Ops:
  0.6 67.7 %shard_map.77 = (bf16[28,48,256]{2,1,0:T(8,128)(2,1)}, bf16[27,24,48]{2,1,0:T(8,128)(2,1)}) custom-call(s32[32]{0:T(128)} %length.1, s32[32]{0:T(128)} %slab.1, s32[32]{0:T(128)} %order.1, bf16[2,8,48,256]{3,2,1,0:T(8,128)(2,1)} %bitcast.1, bf16[28,384,256]{2,1,0:T(8,128)(2,1)} %act.1, bf16[27,384,384]{2,1,0:T(8,128)(2,1)} %w.1), custom_call_target="tpu_custom_call" | custom-call | tf_op jit(solution)/shard_map/pallas_call | solution.py:335
  68.3 2.0 %copy.10 = bf16[28,48,256]{2,1,0:T(8,128)(2,1)} copy(bf16[28,48,256]{2,1,0:T(8,128)(2,1)} %get-tuple-element.4) | data formatting | bytes 1376256
  70.3 1.6 %copy.11 = bf16[27,24,48]{2,1,0:T(8,128)(2,1)} copy(bf16[27,24,48]{2,1,0:T(8,128)(2,1)} %get-tuple-element.5) | data formatting | bytes 124416

commit v2 on v1

--- a/solution.py
+++ b/solution.py
@@ -23,6 +23,7 @@
 NC = 3
 CH = OG // NC
 CLIPS = 32
+CUTS = ((0, 768), (768, 27 * OG))
 SCALE = 1.0 / math.sqrt(256 * PIX)
 
 
@@ -73,7 +74,7 @@
 
 def body(
     length, slab, order, g, act, w, dx, dw,
-    pk, tab, pick, act_v, w_v, rbuf0, rbuf1, rbuf2, qbuf, dbuf0, dbuf1, dbuf2, gs, taps, part, psend, precv, ebuf, hbuf, osend, xbuf,
+    pk, tab, pick, act_v, w_v, rbuf0, rbuf1, rbuf2, qbuf, dbuf0, dbuf1, dbuf2, gs, taps, part, psend0, psend1, precv0, precv1, ebuf, hbuf, osend, xbuf,
     s1, r1, s2, r2, s3, r3, s4, r4, s5, r5, la, lw, lo,
 ):
     ms = lax.axis_index("slab")
@@ -100,6 +101,7 @@
     def piece(d, cs):
         return g.at[:, d // 2, cs, pl.ds(pl.multiple_of((d % 2) * 128, 128), 128)]
 
+    psend, precv = (psend0, psend1), (precv0, precv1)
     rbuf, dbuf = (rbuf0, rbuf1, rbuf2), (dbuf0, dbuf1, dbuf2)
     chunks = [pl.ds(c * CH, CH) for c in range(NC)]
     own = []
@@ -230,28 +232,29 @@
     for cp in loads:
         cp.wait()
     part[...] = jnp.zeros_like(part)
-
-    def mul(n, _):
-        a4 = act_v[:, pl.ds(pl.multiple_of(n * 4 * PIX, 4 * PIX), 4 * PIX)]
-        b4 = taps[:, pl.ds(pl.multiple_of((n * 4 + 2) * PIX, 2 * PIX), 4 * PIX)]
-        part[...] += lax.dot_general(
-            a4, b4, (((1,), (1,)), ((), ())), preferred_element_type=jnp.float32)
-        return 0
-
-    lax.fori_loop(0, SLOTS // 4, mul, 0)
-
     fourth = []
-    for k in list(range(1, NS)) + [0]:
-        d = (ms + k) % NS
-        psend[d] = (part[pl.ds(pl.multiple_of(d * 24, 8), 24), :] * SCALE).astype(jnp.bfloat16)
-        if k:
-            cp = pltpu.make_async_remote_copy(
-                src_ref=psend.at[d], dst_ref=precv.at[ms],
-                send_sem=s4.at[k], recv_sem=r4.at[k],
-                device_id={"slab": d}, device_id_type=MESH)
-            cp.start()
-            fourth.append(cp)
-    precv[ms] = psend[ms]
+    for e, (lo_t, hi_t) in enumerate(CUTS):
+        def mul(n, _):
+            a4 = act_v[:, pl.ds(pl.multiple_of(n * 4 * PIX, 4 * PIX), 4 * PIX)]
+            b4 = taps[lo_t:hi_t, pl.ds(pl.multiple_of((n * 4 + 2) * PIX, 2 * PIX), 4 * PIX)]
+            part[:, lo_t:hi_t] += lax.dot_general(
+                a4, b4, (((1,), (1,)), ((), ())), preferred_element_type=jnp.float32)
+            return 0
+
+        lax.fori_loop(0, SLOTS // 4, mul, 0)
+        for k in list(range(1, NS)) + [0]:
+            d = (ms + k) % NS
+            psend[e][d] = (
+                part[pl.ds(pl.multiple_of(d * 24, 8), 24), lo_t:hi_t] * SCALE
+            ).astype(jnp.bfloat16)
+            if k:
+                cp = pltpu.make_async_remote_copy(
+                    src_ref=psend[e].at[d], dst_ref=precv[e].at[ms],
+                    send_sem=s4.at[e, k], recv_sem=r4.at[e, k],
+                    device_id={"slab": d}, device_id_type=MESH)
+                cp.start()
+                fourth.append(cp)
+        precv[e][ms] = psend[e][ms]
 
     own3.wait()
     for cp in wloads:
@@ -297,13 +300,18 @@
 
     for cp in fourth:
         cp.wait()
-    acc = precv[0].astype(jnp.float32)
-    for s in range(1, NS):
-        acc += precv[s].astype(jnp.float32)
-    acc = acc.astype(jnp.bfloat16)
+    sums = []
+    for e in range(2):
+        acc = precv[e][0].astype(jnp.float32)
+        for k in range(1, NS):
+            acc += precv[e][k].astype(jnp.float32)
+        sums.append(acc.astype(jnp.bfloat16))
     for c in range(NC):
         for t in range(27):
-            dw[t, :, c * CH:(c + 1) * CH] = acc[:, (c * 27 + t) * CH:(c * 27 + t + 1) * CH]
+            at = (c * 27 + t) * CH
+            e = 1 if at >= CUTS[1][0] else 0
+            at -= CUTS[e][0]
+            dw[t, :, c * CH:(c + 1) * CH] = sums[e][:, at:at + CH]
 
     for cp in first + second:
         cp.wait_send()
@@ -352,14 +360,13 @@
             pltpu.VMEM((SLOTS + FD + 2, OG, PIX), bf),
             pltpu.VMEM((27 * OG, (SLOTS + 4) * PIX), bf),
             pltpu.VMEM((C, 27 * OG), jnp.float32),
-            pltpu.VMEM((NS, 24, 27 * OG), bf),
-            pltpu.VMEM((NS, 24, 27 * OG), bf),
+            *[pltpu.VMEM((NS, 24, CUTS[e][1] - CUTS[e][0]), bf) for e in (0, 1, 0, 1)],
             pltpu.VMEM((FD + 2, C, PIX), bf),
             pltpu.VMEM((9 * C, (FD + 2) * PIX), bf),
             pltpu.VMEM((FD, NH, OG, PIX), bf),
             pltpu.VMEM((NH * FD, OG, PIX), bf),
             dma((NC, NS)), dma((NC, NS)), dma((NC, NS)), dma((NC, NS)),
-            dma((NC, NH)), dma((NC, NH)), dma((NS,)), dma((NS,)),
+            dma((NC, NH)), dma((NC, NH)), dma((2, NS)), dma((2, NS)),
             dma((NH, FD)), dma((NH, FD)),
             dma((SLOTS,)), dma((27,)), dma((NC,)),
         ],

time: 72.1 us -> 68.9 us (0.956)
  Pallas kernels: 67.7 us -> 64.5 us
    pallas_call x1, Pallas kernels: 67.7 us -> 64.5 us  [shards(): pl.pallas_call(body, out_shape=(jax.ShapeDtypeStruct((SLOTS, OG, PIX), bf...]
where the time goes in v2:
time: 68.9 us; the launch traced here: 68.7 us
  Pallas kernels  64.5 us (94%)
  local copies, waits for them, and re-layouts  3.59 us (5%)
    pallas_call x1, Pallas kernels, shards(): pl.pallas_call(body, out_shape=(jax.ShapeDtypeStruct((SLOTS, OG, PIX), bf...  64.5 us
    unnamed x2, local copies, waits for them, and re-layouts  3.59 us

profile of v2, /device:TPU:1, one launch (start us, length us, event | category | flops | bytes accessed | tf_op | source)
XLA Modules:
  0.0 68.7 jit_solution(2463017940091629296)
XLA Ops:
  0.6 64.5 %shard_map.77 = (bf16[28,48,256]{2,1,0:T(8,128)(2,1)}, bf16[27,24,48]{2,1,0:T(8,128)(2,1)}) custom-call(s32[32]{0:T(128)} %length.1, s32[32]{0:T(128)} %slab.1, s32[32]{0:T(128)} %order.1, bf16[2,8,48,256]{3,2,1,0:T(8,128)(2,1)} %bitcast.1, bf16[28,384,256]{2,1,0:T(8,128)(2,1)} %act.1, bf16[27,384,384]{2,1,0:T(8,128)(2,1)} %w.1), custom_call_target="tpu_custom_call" | custom-call | tf_op jit(solution)/shard_map/pallas_call | solution.py:343
  65.1 2.0 %copy.10 = bf16[28,48,256]{2,1,0:T(8,128)(2,1)} copy(bf16[28,48,256]{2,1,0:T(8,128)(2,1)} %get-tuple-element.4) | data formatting | bytes 1376256
  67.1 1.6 %copy.11 = bf16[27,24,48]{2,1,0:T(8,128)(2,1)} copy(bf16[27,24,48]{2,1,0:T(8,128)(2,1)} %get-tuple-element.5) | data formatting | bytes 124416

commit v3 on v2

--- a/solution.py
+++ b/solution.py
@@ -23,7 +23,7 @@
 NC = 3
 CH = OG // NC
 CLIPS = 32
-CUTS = ((0, 768), (768, 27 * OG))
+CUTS = ((0, 1024), (1024, 27 * OG))
 SCALE = 1.0 / math.sqrt(256 * PIX)
 
 

time: 68.9 us -> 69.5 us (level)
  no operation moved by 1% of the time
where the time goes in v3:
time: 69.5 us; the launch traced here: 69.3 us
  Pallas kernels  65.1 us (94%)
  local copies, waits for them, and re-layouts  3.59 us (5%)
    pallas_call x1, Pallas kernels, shards(): pl.pallas_call(body, out_shape=(jax.ShapeDtypeStruct((SLOTS, OG, PIX), bf...  65.1 us
    unnamed x2, local copies, waits for them, and re-layouts  3.59 us

profile of v3, /device:TPU:1, one launch (start us, length us, event | category | flops | bytes accessed | tf_op | source)
XLA Modules:
  0.0 69.3 jit_solution(4134202176706017896)
XLA Ops:
  0.6 65.1 %shard_map.77 = (bf16[28,48,256]{2,1,0:T(8,128)(2,1)}, bf16[27,24,48]{2,1,0:T(8,128)(2,1)}) custom-call(s32[32]{0:T(128)} %length.1, s32[32]{0:T(128)} %slab.1, s32[32]{0:T(128)} %order.1, bf16[2,8,48,256]{3,2,1,0:T(8,128)(2,1)} %bitcast.1, bf16[28,384,256]{2,1,0:T(8,128)(2,1)} %act.1, bf16[27,384,384]{2,1,0:T(8,128)(2,1)} %w.1), custom_call_target="tpu_custom_call" | custom-call | tf_op jit(solution)/shard_map/pallas_call | solution.py:343
  65.7 2.0 %copy.10 = bf16[28,48,256]{2,1,0:T(8,128)(2,1)} copy(bf16[28,48,256]{2,1,0:T(8,128)(2,1)} %get-tuple-element.4) | data formatting | bytes 1376256
  67.7 1.6 %copy.11 = bf16[27,24,48]{2,1,0:T(8,128)(2,1)} copy(bf16[27,24,48]{2,1,0:T(8,128)(2,1)} %get-tuple-element.5) | data formatting | bytes 124416
